TPU v7x, 256 devices: a whole 4x4x8 slice. The times are simulated.
256 devices in a mesh: row: 16 (over z_hi, x), col: 16 (over z_lo, y, core).
Axes of the slice: x: 4, y: 4, z: 8 (z_hi: 4, z_lo: 2; z = z_hi * 2 + z_lo), core: 2. Of those that a mesh axis runs over, the one named last changes fastest.
Arguments:
- features: bfloat16 [32768, 1024], P(('col', 'row')), may hold values from -6 to 6
- weight: bfloat16 [1024, 1024], P('col'), may hold values from -0.1875 to 0.1875
- tile_values: bfloat16 [16, 16, 16, 8, 128, 128], P('row', 'col'), may hold values from -0.0625 to 0.0625
- block_cols: int32 [16, 16, 16, 8], P('row', 'col'), may hold values from 0 to 15, as said below
- tile_counts: int32 [16, 16, 16], P('row', 'col'), may hold values from 1 to 8, as said below
Outputs:
- hidden_out: bfloat16 [32768, 1024], P(('row', 'col'))
Inputs may be any that keep to these rules, and one draw needn't show every extreme that they name: `block_cols`: the 8 entries of one block row of a tile are distinct block columns; values and block columns of slots that are not live are arbitrary. `tile_counts`: every tile has a block row with all 8 slots live.
All inputs are finite; a program needn't handle non-finite values.
Results may differ from a plain program's by a relative error of at most 0.019.
Values may be sent and summed in bfloat16 or wider, within the bound.
No kernel may reach another device: no remote copies, remote signals or barrier semaphores. Data moves between devices by JAX's collectives and lax.ppermute only.
A program may use at most 64 MiB of HBM per device.

v0:
```python
from functools import partial
import jax
import jax.numpy as jnp
from jax import lax
from jax.sharding import PartitionSpec as P


def aggregate(slot_values, slot_cols, slot_count, column_rows, group_size, offset, row_span):
    block_size = slot_values.shape[-1]
    slot_total = slot_values.shape[1]
    feat_width = column_rows.shape[-1]
    by_block = column_rows.reshape(-1, block_size, feat_width)
    row_count = row_span // block_size
    values_part = slot_values
    cols_part = slot_cols
    count_part = slot_count
    groups = row_count // group_size
    values_part = values_part.reshape(groups, group_size, slot_total, block_size, block_size)
    cols_part = cols_part.reshape(groups, group_size, slot_total)
    count_part = count_part.reshape(groups, group_size)

    def one_group(group_args):
        group_values, group_cols, group_count = group_args
        gathered = by_block[group_cols]
        live_slots = jnp.arange(slot_total, dtype=jnp.int32)[None, :] < group_count[:, None]
        masked = jnp.where(live_slots[:, :, None, None], group_values, jnp.zeros_like(group_values))
        return jnp.einsum("rsab,rsbf->raf", masked, gathered, preferred_element_type=jnp.float32)

    result = lax.map(one_group, (values_part, cols_part, count_part))
    return result.reshape(row_span, feat_width)


def body(features, weight, tile_values, block_cols, tile_counts):
    slot_values = tile_values[0, 0]
    slot_cols = block_cols[0, 0]
    slot_count = tile_counts[0, 0]
    out_rows = features.shape[0]
    block_size = slot_values.shape[-1]
    group_size = out_rows // block_size
    column_rows = lax.all_gather(features, "row", axis=0, tiled=True)
    partial_term = partial(aggregate, slot_values, slot_cols, slot_count, column_rows, group_size)
    summed = lax.psum_scatter(
        partial_term(jnp.int32(0), lax.axis_size("col") * out_rows).astype(jnp.bfloat16),
        "col",
        scatter_dimension=0,
        tiled=True,
    )
    product = jnp.dot(
        summed,
        lax.all_gather(weight, "col", axis=0, tiled=True),
        preferred_element_type=jnp.float32,
    )
    return jnp.maximum(product, 0.0).astype(jnp.bfloat16)


def solution(mesh):
    in_specs = (
        P(("col", "row"), None),
        P("col", None),
        P("row", "col", None, None, None, None),
        P("row", "col", None, None),
        P("row", "col", None),
    )
    out_specs = P(("row", "col"), None)
    return jax.shard_map(body, mesh=mesh, in_specs=in_specs, out_specs=out_specs, check_vma=False)
```

profile of v0, /device:TPU:2, one launch (start us, length us, event | category | flops | bytes accessed | tf_op | source)
XLA Modules:
  0.0 268.3 jit_solution(4133239872601638736)
XLA Ops:
  8.8 78.9 %all-gather.3.cloned.1.call-done = bf16[2048,1024]{1,0:T(8,128)(2,1)} async-done(((bf16[128,1024]{1,0:T(8,128)(2,1)}), bf16[2048,1024]{1,0:T(8,128)(2,1)}) %all-gather.3.cloned.1.call-update) | async-done | bytes 4194320 | tf_op jit(solution)/shard_map/all_gather | solution.py:40
  87.7 100.7 %while.10 = (s32[]{:T(128)}, bf16[16,1,128,1024]{3,2,1,0:T(8,128)(2,1)}, s32[16,1]{0,1:T(1,128)}, bf16[16,1,8,128,128]{4,3,2,1,0:T(8,128)(2,1)}, s32[16,1,8]{2,1...) while((s32[]{:T(128)}, bf16[16,1,128,1024]{3,2,1,0:T(8,128)(2,1)}, s32[16,1]{0,1:T(1,128)}, ...), condition=%wide.region_1.2_spmd, body=%wide.region_0.1_spmd.sunk | while | flops 268567584 | bytes 7083533 | solution.py:29
  87.7 2.9 %gather_fusion = bf16[8,128,1024]{2,1,0:T(8,128)(2,1)S(1)} fusion(bf16[16,128,1024]{2,1,0:T(8,128)(2,1)} %get-tuple-element.112, s32[1024]{0:T(1024)S(1)} %pad_clamp_fusion.2), kind=kCustom, calls=%fused_computation.clone.1 | custom fusion | bytes 4194336 | tf_op jit(solution)/shard_map/while/body/eval_jaxpr/gather | solution.py:24
  91.8 2.2 fusion.17
  94.0 2.9 %gather_fusion = bf16[8,128,1024]{2,1,0:T(8,128)(2,1)S(1)} fusion(bf16[16,128,1024]{2,1,0:T(8,128)(2,1)} %get-tuple-element.112, s32[1024]{0:T(1024)S(1)} %pad_clamp_fusion.2), kind=kCustom, calls=%fused_computation.clone.1 | custom fusion | bytes 4194336 | tf_op jit(solution)/shard_map/while/body/eval_jaxpr/gather | solution.py:24
  98.1 2.2 fusion.17
  100.3 3.0 %gather_fusion = bf16[8,128,1024]{2,1,0:T(8,128)(2,1)S(1)} fusion(bf16[16,128,1024]{2,1,0:T(8,128)(2,1)} %get-tuple-element.112, s32[1024]{0:T(1024)S(1)} %pad_clamp_fusion.2), kind=kCustom, calls=%fused_computation.clone.1 | custom fusion | bytes 4194336 | tf_op jit(solution)/shard_map/while/body/eval_jaxpr/gather | solution.py:24
  104.5 2.2 fusion.17
  106.7 2.9 %gather_fusion = bf16[8,128,1024]{2,1,0:T(8,128)(2,1)S(1)} fusion(bf16[16,128,1024]{2,1,0:T(8,128)(2,1)} %get-tuple-element.112, s32[1024]{0:T(1024)S(1)} %pad_clamp_fusion.2), kind=kCustom, calls=%fused_computation.clone.1 | custom fusion | bytes 4194336 | tf_op jit(solution)/shard_map/while/body/eval_jaxpr/gather | solution.py:24
  110.8 2.2 fusion.17
  113.0 2.9 %gather_fusion = bf16[8,128,1024]{2,1,0:T(8,128)(2,1)S(1)} fusion(bf16[16,128,1024]{2,1,0:T(8,128)(2,1)} %get-tuple-element.112, s32[1024]{0:T(1024)S(1)} %pad_clamp_fusion.2), kind=kCustom, calls=%fused_computation.clone.1 | custom fusion | bytes 4194336 | tf_op jit(solution)/shard_map/while/body/eval_jaxpr/gather | solution.py:24
  117.1 2.2 fusion.17
  119.3 2.9 %gather_fusion = bf16[8,128,1024]{2,1,0:T(8,128)(2,1)S(1)} fusion(bf16[16,128,1024]{2,1,0:T(8,128)(2,1)} %get-tuple-element.112, s32[1024]{0:T(1024)S(1)} %pad_clamp_fusion.2), kind=kCustom, calls=%fused_computation.clone.1 | custom fusion | bytes 4194336 | tf_op jit(solution)/shard_map/while/body/eval_jaxpr/gather | solution.py:24
  123.4 2.2 fusion.17
  125.6 2.9 %gather_fusion = bf16[8,128,1024]{2,1,0:T(8,128)(2,1)S(1)} fusion(bf16[16,128,1024]{2,1,0:T(8,128)(2,1)} %get-tuple-element.112, s32[1024]{0:T(1024)S(1)} %pad_clamp_fusion.2), kind=kCustom, calls=%fused_computation.clone.1 | custom fusion | bytes 4194336 | tf_op jit(solution)/shard_map/while/body/eval_jaxpr/gather | solution.py:24
  131.8 2.9 %gather_fusion = bf16[8,128,1024]{2,1,0:T(8,128)(2,1)S(1)} fusion(bf16[16,128,1024]{2,1,0:T(8,128)(2,1)} %get-tuple-element.112, s32[1024]{0:T(1024)S(1)} %pad_clamp_fusion.2), kind=kCustom, calls=%fused_computation.clone.1 | custom fusion | bytes 4194336 | tf_op jit(solution)/shard_map/while/body/eval_jaxpr/gather | solution.py:24
  138.1 2.9 %gather_fusion = bf16[8,128,1024]{2,1,0:T(8,128)(2,1)S(1)} fusion(bf16[16,128,1024]{2,1,0:T(8,128)(2,1)} %get-tuple-element.112, s32[1024]{0:T(1024)S(1)} %pad_clamp_fusion.2), kind=kCustom, calls=%fused_computation.clone.1 | custom fusion | bytes 4194336 | tf_op jit(solution)/shard_map/while/body/eval_jaxpr/gather | solution.py:24
  142.2 2.1 fusion.17
  144.4 2.9 %gather_fusion = bf16[8,128,1024]{2,1,0:T(8,128)(2,1)S(1)} fusion(bf16[16,128,1024]{2,1,0:T(8,128)(2,1)} %get-tuple-element.112, s32[1024]{0:T(1024)S(1)} %pad_clamp_fusion.2), kind=kCustom, calls=%fused_computation.clone.1 | custom fusion | bytes 4194336 | tf_op jit(solution)/shard_map/while/body/eval_jaxpr/gather | solution.py:24
  148.5 2.2 fusion.17
  150.7 2.9 %gather_fusion = bf16[8,128,1024]{2,1,0:T(8,128)(2,1)S(1)} fusion(bf16[16,128,1024]{2,1,0:T(8,128)(2,1)} %get-tuple-element.112, s32[1024]{0:T(1024)S(1)} %pad_clamp_fusion.2), kind=kCustom, calls=%fused_computation.clone.1 | custom fusion | bytes 4194336 | tf_op jit(solution)/shard_map/while/body/eval_jaxpr/gather | solution.py:24
  154.8 2.2 fusion.17
  156.9 2.9 %gather_fusion = bf16[8,128,1024]{2,1,0:T(8,128)(2,1)S(1)} fusion(bf16[16,128,1024]{2,1,0:T(8,128)(2,1)} %get-tuple-element.112, s32[1024]{0:T(1024)S(1)} %pad_clamp_fusion.2), kind=kCustom, calls=%fused_computation.clone.1 | custom fusion | bytes 4194336 | tf_op jit(solution)/shard_map/while/body/eval_jaxpr/gather | solution.py:24
  161.1 2.2 fusion.17
  163.2 2.9 %gather_fusion = bf16[8,128,1024]{2,1,0:T(8,128)(2,1)S(1)} fusion(bf16[16,128,1024]{2,1,0:T(8,128)(2,1)} %get-tuple-element.112, s32[1024]{0:T(1024)S(1)} %pad_clamp_fusion.2), kind=kCustom, calls=%fused_computation.clone.1 | custom fusion | bytes 4194336 | tf_op jit(solution)/shard_map/while/body/eval_jaxpr/gather | solution.py:24
  167.4 2.2 fusion.17
  169.5 2.9 %gather_fusion = bf16[8,128,1024]{2,1,0:T(8,128)(2,1)S(1)} fusion(bf16[16,128,1024]{2,1,0:T(8,128)(2,1)} %get-tuple-element.112, s32[1024]{0:T(1024)S(1)} %pad_clamp_fusion.2), kind=kCustom, calls=%fused_computation.clone.1 | custom fusion | bytes 4194336 | tf_op jit(solution)/shard_map/while/body/eval_jaxpr/gather | solution.py:24
  175.8 2.9 %gather_fusion = bf16[8,128,1024]{2,1,0:T(8,128)(2,1)S(1)} fusion(bf16[16,128,1024]{2,1,0:T(8,128)(2,1)} %get-tuple-element.112, s32[1024]{0:T(1024)S(1)} %pad_clamp_fusion.2), kind=kCustom, calls=%fused_computation.clone.1 | custom fusion | bytes 4194336 | tf_op jit(solution)/shard_map/while/body/eval_jaxpr/gather | solution.py:24
  182.1 2.9 %gather_fusion = bf16[8,128,1024]{2,1,0:T(8,128)(2,1)S(1)} fusion(bf16[16,128,1024]{2,1,0:T(8,128)(2,1)} %get-tuple-element.112, s32[1024]{0:T(1024)S(1)} %pad_clamp_fusion.2), kind=kCustom, calls=%fused_computation.clone.1 | custom fusion | bytes 4194336 | tf_op jit(solution)/shard_map/while/body/eval_jaxpr/gather | solution.py:24
  186.2 2.2 fusion.17
  188.4 70.5 %reduce-scatter.2.cloned.1.call-done = bf16[128,1024]{1,0:T(8,128)(2,1)} async-done(((bf16[2048,1024]{1,0:T(8,128)(2,1)}), bf16[128,1024]{1,0:T(8,128)(2,1)}) %reduce-scatter.2.cloned.1.call-update) | async-done | bytes 262160 | tf_op jit(solution)/shard_map/reduce_scatter | solution.py:42
  258.9 2.8 %fusion.8 = bf16[128,1024]{1,0:T(8,128)(2,1)} fusion(bf16[128,1024]{1,0:T(8,128)(2,1)} %reduce-scatter.2.cloned.1.call-done, bf16[1024,1024]{1,0:T(8,128)(2,1)} %all-gather.5.cloned.1.call-done), kind=kOutput, calls=%fused_computation.17 | convolution fusion | flops 268697600 | bytes 2621440 | tf_op jit(solution)/shard_map/dot_general | solution.py:48
  (109 shorter events, 30.5 us)
Async XLA Ops:
  6.5 81.2 %all-gather.3.cloned.1.call-start = ((), (), s32[]{:S(2)}) async-start(), calls=%async_computation.1 | async-start | bytes 4456448 | tf_op jit(solution)/shard_map/all_gather | solution.py:40
  7.3 181.2 %all-gather.5.cloned.1.call-start = ((), (), s32[]{:S(2)}) async-start(), calls=%async_computation.3 | async-start | bytes 2228224 | tf_op jit(solution)/shard_map/all_gather | solution.py:50
  8.0 250.9 %reduce-scatter.2.cloned.1.call-start = ((), (), s32[]{:S(2)}) async-start(), calls=%async_computation.2 | async-start | bytes 4456448 | tf_op jit(solution)/shard_map/reduce_scatter | solution.py:42
  87.7 2.9 %copy-start = (s32[16,1]{0,1:T(1,128)S(1)}, s32[16,1]{0,1:T(1,128)}, u32[]{:S(2)}) copy-start(s32[16,1]{0,1:T(1,128)} %get-tuple-element.109) | copy-start | bytes 196 | tf_op jit(solution)/shard_map/while
  94.0 2.9 %copy-start = (s32[16,1]{0,1:T(1,128)S(1)}, s32[16,1]{0,1:T(1,128)}, u32[]{:S(2)}) copy-start(s32[16,1]{0,1:T(1,128)} %get-tuple-element.109) | copy-start | bytes 196 | tf_op jit(solution)/shard_map/while
  100.3 3.0 %copy-start = (s32[16,1]{0,1:T(1,128)S(1)}, s32[16,1]{0,1:T(1,128)}, u32[]{:S(2)}) copy-start(s32[16,1]{0,1:T(1,128)} %get-tuple-element.109) | copy-start | bytes 196 | tf_op jit(solution)/shard_map/while
  106.7 2.9 %copy-start = (s32[16,1]{0,1:T(1,128)S(1)}, s32[16,1]{0,1:T(1,128)}, u32[]{:S(2)}) copy-start(s32[16,1]{0,1:T(1,128)} %get-tuple-element.109) | copy-start | bytes 196 | tf_op jit(solution)/shard_map/while
  113.0 2.9 %copy-start = (s32[16,1]{0,1:T(1,128)S(1)}, s32[16,1]{0,1:T(1,128)}, u32[]{:S(2)}) copy-start(s32[16,1]{0,1:T(1,128)} %get-tuple-element.109) | copy-start | bytes 196 | tf_op jit(solution)/shard_map/while
  119.3 2.9 %copy-start = (s32[16,1]{0,1:T(1,128)S(1)}, s32[16,1]{0,1:T(1,128)}, u32[]{:S(2)}) copy-start(s32[16,1]{0,1:T(1,128)} %get-tuple-element.109) | copy-start | bytes 196 | tf_op jit(solution)/shard_map/while
  125.6 2.9 %copy-start = (s32[16,1]{0,1:T(1,128)S(1)}, s32[16,1]{0,1:T(1,128)}, u32[]{:S(2)}) copy-start(s32[16,1]{0,1:T(1,128)} %get-tuple-element.109) | copy-start | bytes 196 | tf_op jit(solution)/shard_map/while
  131.8 2.9 %copy-start = (s32[16,1]{0,1:T(1,128)S(1)}, s32[16,1]{0,1:T(1,128)}, u32[]{:S(2)}) copy-start(s32[16,1]{0,1:T(1,128)} %get-tuple-element.109) | copy-start | bytes 196 | tf_op jit(solution)/shard_map/while
  138.1 2.9 %copy-start = (s32[16,1]{0,1:T(1,128)S(1)}, s32[16,1]{0,1:T(1,128)}, u32[]{:S(2)}) copy-start(s32[16,1]{0,1:T(1,128)} %get-tuple-element.109) | copy-start | bytes 196 | tf_op jit(solution)/shard_map/while
  144.4 2.9 %copy-start = (s32[16,1]{0,1:T(1,128)S(1)}, s32[16,1]{0,1:T(1,128)}, u32[]{:S(2)}) copy-start(s32[16,1]{0,1:T(1,128)} %get-tuple-element.109) | copy-start | bytes 196 | tf_op jit(solution)/shard_map/while
  150.6 2.9 %copy-start = (s32[16,1]{0,1:T(1,128)S(1)}, s32[16,1]{0,1:T(1,128)}, u32[]{:S(2)}) copy-start(s32[16,1]{0,1:T(1,128)} %get-tuple-element.109) | copy-start | bytes 196 | tf_op jit(solution)/shard_map/while
  156.9 2.9 %copy-start = (s32[16,1]{0,1:T(1,128)S(1)}, s32[16,1]{0,1:T(1,128)}, u32[]{:S(2)}) copy-start(s32[16,1]{0,1:T(1,128)} %get-tuple-element.109) | copy-start | bytes 196 | tf_op jit(solution)/shard_map/while
  163.2 2.9 %copy-start = (s32[16,1]{0,1:T(1,128)S(1)}, s32[16,1]{0,1:T(1,128)}, u32[]{:S(2)}) copy-start(s32[16,1]{0,1:T(1,128)} %get-tuple-element.109) | copy-start | bytes 196 | tf_op jit(solution)/shard_map/while
  169.5 2.9 %copy-start = (s32[16,1]{0,1:T(1,128)S(1)}, s32[16,1]{0,1:T(1,128)}, u32[]{:S(2)}) copy-start(s32[16,1]{0,1:T(1,128)} %get-tuple-element.109) | copy-start | bytes 196 | tf_op jit(solution)/shard_map/while
  175.8 2.9 %copy-start = (s32[16,1]{0,1:T(1,128)S(1)}, s32[16,1]{0,1:T(1,128)}, u32[]{:S(2)}) copy-start(s32[16,1]{0,1:T(1,128)} %get-tuple-element.109) | copy-start | bytes 196 | tf_op jit(solution)/shard_map/while
  182.0 2.9 %copy-start = (s32[16,1]{0,1:T(1,128)S(1)}, s32[16,1]{0,1:T(1,128)}, u32[]{:S(2)}) copy-start(s32[16,1]{0,1:T(1,128)} %get-tuple-element.109) | copy-start | bytes 196 | tf_op jit(solution)/shard_map/while
Sparse Core Ops, SparseCore 0:
  9.8 77.9 all-gather.2
  89.6 36.9 all-gather.4
  188.5 70.3 reduce-scatter.1
where the time goes:
time: 269 us; the launch traced here: 268 us
  waiting for transfers between devices  151 us (56%)
  local copies, waits for them, and re-layouts  56.3 us (21%)
  matrix products  37.4 us (14%)
  between operations  13.1 us (5%)
  other arithmetic  10.1 us (4%)
    all_gather x1, waiting for transfers between devices, body(): column_rows = lax.all_gather(features, 'row', axis=0, tiled=True)  78.9 us
    reduce_scatter x1, waiting for transfers between devices, body(): lax.psum_scatter(partial_term(jnp.int32(0), lax.axis_size('col') * out_ro...  70.5 us
    gather x16, local copies, waits for them, and re-layouts, one_group(): gathered = by_block[group_cols]  46 us
    dot_general x16, matrix products, one_group(): jnp.einsum('rsab,rsbf->raf', masked, gathered, preferred_element_type=jnp...  34.6 us
    lt x16, other arithmetic, one_group(): jnp.arange(slot_total, dtype=jnp.int32)[None, :] < group_count[:, None]  9.91 us
    dynamic_slice x16, local copies, waits for them, and re-layouts, aggregate(): result = lax.map(one_group, (values_part, cols_part, count_part))  9.52 us
  transfers between devices with their start and end apart: 3, of which 2 were waited for; matrix products, arithmetic and copies ran while one was open for 38% of the time, Pallas kernels for 0%

commit v1 on v0

--- a/solution.py
+++ b/solution.py
@@ -37,7 +37,9 @@
     out_rows = features.shape[0]
     block_size = slot_values.shape[-1]
     group_size = out_rows // block_size
-    column_rows = lax.all_gather(features, "row", axis=0, tiled=True)
+    column_rows = jnp.concatenate(
+        lax.all_to_all(jnp.stack([features] * lax.axis_size("row")), "row", 0, 0), axis=0
+    )
     partial_term = partial(aggregate, slot_values, slot_cols, slot_count, column_rows, group_size)
     summed = lax.psum_scatter(
         partial_term(jnp.int32(0), lax.axis_size("col") * out_rows).astype(jnp.bfloat16),

time: 269 us -> 306 us (1.14)
  waiting for transfers between devices: 151 us -> 172 us
  starting transfers between devices: 0.08 us -> 11.7 us
    all_to_all x0 -> x1, waiting for transfers between devices: none -> 104 us  [body(): lax.all_to_all(jnp.stack([features] * lax.axis_size('row')), 'row', 0, 0)]
    all_gather x1 -> x0, waiting for transfers between devices: 78.9 us -> none  [body(): column_rows = lax.all_gather(features, 'row', axis=0, tiled=True)]
    all_to_all x0 -> x1, starting transfers between devices: none -> 11.6 us  [body(): lax.all_to_all(jnp.stack([features] * lax.axis_size('row')), 'row', 0, 0)]
    another operation x0 -> x1, local copies, waits for them, and re-layouts: none -> 3.46 us  [body(): jnp.stack([features] * lax.axis_size('row'))]
    reduce_scatter x1, waiting for transfers between devices: 70.5 us -> 67 us  [body(): lax.psum_scatter(partial_term(jnp.int32(0), lax.axis_size('col') * out_ro...]
  transfers between devices with their start and end apart: 3 -> 3, of which waited for: 2 -> 2; matrix products, arithmetic and copies ran while one was open for 38% -> 33% of each run, Pallas kernels for 0% -> 0%
where the time goes in v1:
time: 306 us; the launch traced here: 304 us
  waiting for transfers between devices  172 us (56%)
  local copies, waits for them, and re-layouts  59 us (19%)
  matrix products  37.4 us (12%)
  between operations  13.4 us (4%)
  starting transfers between devices  11.7 us (4%)
  other arithmetic  10.1 us (3%)
    all_to_all x1, waiting for transfers between devices, body(): lax.all_to_all(jnp.stack([features] * lax.axis_size('row')), 'row', 0, 0)  104 us
    reduce_scatter x1, waiting for transfers between devices, body(): lax.psum_scatter(partial_term(jnp.int32(0), lax.axis_size('col') * out_ro...  67 us
    gather x16, local copies, waits for them, and re-layouts, one_group(): gathered = by_block[group_cols]  45.9 us
    dot_general x16, matrix products, one_group(): jnp.einsum('rsab,rsbf->raf', masked, gathered, preferred_element_type=jnp...  34.6 us
    all_to_all x1, starting transfers between devices, body(): lax.all_to_all(jnp.stack([features] * lax.axis_size('row')), 'row', 0, 0)  11.6 us
    lt x16, other arithmetic, one_group(): jnp.arange(slot_total, dtype=jnp.int32)[None, :] < group_count[:, None]  9.96 us
    dynamic_slice x16, local copies, waits for them, and re-layouts, aggregate(): result = lax.map(one_group, (values_part, cols_part, count_part))  9.57 us
  transfers between devices with their start and end apart: 3, of which 2 were waited for; matrix products, arithmetic and copies ran while one was open for 33% of the time, Pallas kernels for 0%

profile of v1, /device:TPU:2, one launch (start us, length us, event | category | flops | bytes accessed | tf_op | source)
XLA Modules:
  0.0 304.1 jit_solution(18159632477161310236)
XLA Ops:
  6.5 3.5 %stack.2 = bf16[16,128,1024]{2,1,0:T(8,128)(2,1)} broadcast(bf16[128,1024]{1,0:T(8,128)(2,1)} %param.7), dimensions={1,2} | broadcast | bytes 4456448 | tf_op jit(solution)/shard_map/stack | solution.py:41
  10.0 11.6 %all-to-all-start = ((bf16[16,128,1024]{2,1,0:T(8,128)(2,1)}), bf16[16,128,1024]{2,1,0:T(8,128)(2,1)}, u32[]{:S(2)}, u32[]{:S(2)}) async-start(bf16[16,128,1024]{2,1,0:T(8,128)(2,1)} %stack.2), calls=%async_computation | async-start | bytes 8388608 | tf_op jit(solution)/shard_map/all_to_all | solution.py:41
  22.5 104.4 %all-to-all-done = bf16[16,128,1024]{2,1,0:T(8,128)(2,1)} async-done(((bf16[16,128,1024]{2,1,0:T(8,128)(2,1)}), bf16[16,128,1024]{2,1,0:T(8,128)(2,1)}, u32[]{:S(2)}, u32[]{:S(2)}) %all-to-all-start) | async-done | bytes 4194336 | tf_op jit(solution)/shard_map/all_to_all | solution.py:41
  126.9 100.4 %while.10 = (s32[]{:T(128)}, bf16[16,1,128,1024]{3,2,1,0:T(8,128)(2,1)}, s32[16,1]{0,1:T(1,128)S(1)}, bf16[16,1,8,128,128]{4,3,2,1,0:T(8,128)(2,1)}, s32[16,1,8]...) while((s32[]{:T(128)}, bf16[16,1,128,1024]{3,2,1,0:T(8,128)(2,1)}, s32[16,1]{0,1:T(1,128)S(1)}, ...), condition=%wide.region_1.2_spmd, body=%wide.region_0.1_spmd.sunk | while | flops 268567584 | bytes 7083249 | solution.py:29
  126.9 2.9 gather_fusion
  131.0 2.2 fusion.17
  133.2 2.9 gather_fusion
  137.3 2.2 fusion.17
  139.5 2.9 gather_fusion
  143.6 2.2 fusion.17
  145.8 2.9 gather_fusion
  149.9 2.2 fusion.17
  152.0 2.9 gather_fusion
  158.3 2.9 gather_fusion
  162.4 2.2 fusion.17
  164.6 2.9 gather_fusion
  170.9 2.9 gather_fusion
  175.0 2.2 fusion.17
  177.1 2.9 gather_fusion
  181.2 2.2 fusion.17
  183.4 2.9 gather_fusion
  189.7 2.9 gather_fusion
  193.8 2.2 fusion.17
  196.0 2.9 gather_fusion
  202.2 2.9 gather_fusion
  206.3 2.2 fusion.17
  208.5 2.9 gather_fusion
  214.8 2.9 gather_fusion
  221.0 2.9 gather_fusion
  225.2 2.2 fusion.17
  227.4 67.0 %reduce-scatter.2.cloned.1.call-done = bf16[128,1024]{1,0:T(8,128)(2,1)} async-done(((bf16[2048,1024]{1,0:T(8,128)(2,1)}), bf16[128,1024]{1,0:T(8,128)(2,1)}) %reduce-scatter.2.cloned.1.call-update) | async-done | bytes 262160 | tf_op jit(solution)/shard_map/reduce_scatter | solution.py:44
  294.4 2.8 fusion.8
  (81 shorter events, 33.5 us)
Async XLA Ops:
  10.0 12.4 %copy-start = (s32[1,1,16,8]{2,3,1,0:T(8,128)S(1)}, s32[1,1,16,8]{2,3,1,0:T(8,128)}, u32[]{:S(2)}) copy-start(s32[1,1,16,8]{2,3,1,0:T(8,128)} %param.10) | copy-start | bytes 1540
  10.0 116.9 %copy-start.1 = (s32[1,1,16]{2,1,0:T(1,128)S(1)}, s32[1,1,16]{2,1,0:T(1,128)}, u32[]{:S(2)}) copy-start(s32[1,1,16]{2,1,0:T(1,128)} %param.11) | copy-start | bytes 196
  10.0 116.9 %all-to-all-start = ((bf16[16,128,1024]{2,1,0:T(8,128)(2,1)}), bf16[16,128,1024]{2,1,0:T(8,128)(2,1)}, u32[]{:S(2)}, u32[]{:S(2)}) async-start(bf16[16,128,1024]{2,1,0:T(8,128)(2,1)} %stack.2), calls=%async_computation | async-start | bytes 8388608 | tf_op jit(solution)/shard_map/all_to_all | solution.py:41
  21.6 205.8 %all-gather.2.cloned.1.call-start = ((), (), s32[]{:S(2)}) async-start(), calls=%async_computation.3 | async-start | bytes 2228224 | tf_op jit(solution)/shard_map/all_gather | solution.py:52
  22.3 272.1 %reduce-scatter.2.cloned.1.call-start = ((), (), s32[]{:S(2)}) async-start(), calls=%async_computation.2 | async-start | bytes 4456448 | tf_op jit(solution)/shard_map/reduce_scatter | solution.py:44
Sparse Core Ops, SparseCore 0:
  24.3 64.3 all-gather.1
  227.5 66.9 reduce-scatter.1
